TPU v7x, 256 devices: a whole 4x4x8 slice. The times are simulated.
256 devices in a mesh: rows: 16 (over z_lo, y, core), tm: 16 (over x, z_hi).
Axes of the slice: x: 4, y: 4, z: 8 (z_hi: 4, z_lo: 2; z = z_hi * 2 + z_lo), core: 2. Of those that a mesh axis runs over, the one named last changes fastest.
Arguments:
- residual: float32 [64, 1024, 512], P('tm', 'rows'), may hold values from -45 to 45
- cycle_weight: float32 [64, 1024, 512], P('tm', 'rows'), may hold values from -0.75 to 0.75
- cycle_offsets: int32 [64, 2], replicated, may hold values from -6 to 6, as said below
Outputs:
- new_weight: float32 [64, 1024, 512], P('tm', 'rows')
- error: float32 [64, 1024, 512], P('tm', 'rows')
Inputs may be any that keep to these rules, and one draw needn't show every extreme that they name: `cycle_offsets`: each row is a distinct (row, column) offset; together the rows are the 64 pixels (dy, dx) with 17 <= dy*dy + dx*dx <= 36, in an order drawn from the seed.
All inputs are finite; a program needn't handle non-finite values.
Results may differ from a plain program's by a relative error of at most 0.0003.
Values sent between devices are 32-bit elements; how exact they have to be, the bound alone decides.
A program may use at most 64 MiB of HBM per device.

v0:
```python
import jax
import jax.numpy as jnp
import numpy as np
from jax import lax
from jax.sharding import PartitionSpec as P


def with_halo(cells, sides, width):
    for axis, dim in sides:
        count = lax.axis_size(axis)
        ends = count - 1
        head = lax.slice_in_dim(cells, 0, width, axis=dim)
        tail = lax.slice_in_dim(cells, cells.shape[dim] - width, cells.shape[dim], axis=dim)
        cells = jnp.concatenate(
            [
                lax.ppermute(tail, axis, [(i, (i + 1) % count) for i in range(ends)]),
                cells,
                lax.ppermute(head, axis, [((i + 1) % count, i) for i in range(ends)]),
            ],
            axis=dim,
        )
    return cells


def cycle_points():
    points = []
    for row_off in range(-6, 7):
        for col_off in range(-6, 7):
            radius = row_off * row_off + col_off * col_off
            if radius >= 17 and radius <= 36:
                points.append((row_off, col_off))
    return points


def matching(cycle_offsets, points):
    table_rows = jnp.asarray(np.array([p[0] for p in points], dtype=np.int32))
    table_cols = jnp.asarray(np.array([p[1] for p in points], dtype=np.int32))
    same = (table_rows[:, None] == cycle_offsets[None, :, 0]) & (
        table_cols[:, None] == cycle_offsets[None, :, 1]
    )
    return same.astype(jnp.float32)


def reorder(selector, weights):
    return jnp.einsum("jk,kyx->jyx", selector, weights, precision=lax.Precision.HIGHEST)


def window_of(padded, point, height, width):
    return padded[:, 6 + point[0] : 6 + point[0] + height, 6 + point[1] : 6 + point[1] + width]


def cycle_passes(padded, centre, ordered_weight, points, height, width):
    background = jnp.zeros(centre.shape, jnp.float32)
    for index, point in enumerate(points):
        background = background + ordered_weight[index][None] * window_of(
            padded, point, height, width
        )
    error_part = centre - background
    grads = jnp.stack(
        [jnp.sum(error_part * window_of(padded, point, height, width), axis=0) for point in points]
    )
    squares = jnp.sum(padded * padded, axis=0)
    energy_sum = jnp.zeros((height, width), jnp.float32)
    for point in points:
        energy_sum = (
            energy_sum
            + squares[6 + point[0] : 6 + point[0] + height, 6 + point[1] : 6 + point[1] + width]
        )
    return (error_part, grads, energy_sum)


def on_device(residual, cycle_weight, cycle_offsets):
    frames_dev, rows_dev, cols = residual.shape
    cycle = cycle_offsets.shape[0]
    tm_count = lax.axis_size("tm")
    frames_all = frames_dev * tm_count
    points = cycle_points()
    selector = matching(cycle_offsets, points)
    extended = with_halo(residual, (("rows", 1),), 6)
    padded = jnp.pad(extended, ((0, 0), (0, 0), (6, 6)))
    columns = selector
    ordered_weight = reorder(columns, lax.all_gather(cycle_weight, "tm", axis=0, tiled=True))
    error, ordered_grad, local_energy = cycle_passes(
        padded, residual, ordered_weight, points, rows_dev, cols
    )
    columns = selector
    gradient = lax.psum_scatter(
        jnp.einsum("jk,jyx->kyx", columns, ordered_grad, precision=lax.Precision.HIGHEST),
        "tm",
        scatter_dimension=0,
        tiled=True,
    )
    energy = lax.psum(local_energy, "tm") / (cycle * frames_all) + 1e-06
    new_weight = cycle_weight + gradient / (frames_all * energy)[None]
    return (new_weight, error)


def solution(mesh):
    in_specs = (P("tm", "rows", None), P("tm", "rows", None), P())
    out_specs = (P("tm", "rows", None), P("tm", "rows", None))
    return jax.shard_map(
        on_device, mesh=mesh, in_specs=in_specs, out_specs=out_specs, check_vma=False
    )
```

profile of v0, /device:TPU:4, one launch (start us, length us, event | category | flops | bytes accessed | tf_op | source)
XLA Modules:
  0.0 429.7 jit_solution(9261241765014633690)
XLA Ops:
  8.0 0.9 fusion.19
  8.9 1.7 collective-permute-start
  10.6 1.3 collective-permute-start.1
  11.9 0.8 slice_bitcast_fusion.1
  12.7 1.1 constant_dynamic-update-slice_fusion.1
  13.8 1.4 collective-permute-done.1
  15.1 1.4 multiply_reduce_fusion
  16.5 2.8 slice_add_fusion
  19.9 97.1 %all-gather.2.cloned.1.call-done = f32[64,64,512]{2,1,0:T(8,128)} async-done(((f32[4,64,512]{2,1,0:T(8,128)}), f32[64,64,512]{2,1,0:T(8,128)}) %all-gather.2.cloned.1.call-update) | async-done | bytes 8388624 | tf_op jit(solution)/shard_map/all_gather | solution.py:82
  117.0 13.4 %fusion = f32[64,64,512]{2,0,1:T(8,128)S(1)} fusion(f32[64,64,512]{2,1,0:T(8,128)} %all-gather.2.cloned.1.call-done, s32[64]{0:T(128)S(1)} %copy-done.4, s32[64]{0:T(128)S(1)} %copy-done.3, s32[64]{0:T(128)S(1)} %get-tuple-element.146, s32[64]{0:T(128)S(1)} %get-tuple-element.145), kind=kOutput, calls=%fused_computation | convolution fusion | flops 1610625024 | bytes 16778240 | tf_op jit(solution)/shard_map/jk,kyx->jyx/dot_general | solution.py:45
  130.5 2.0 fusion.17
  132.4 2.3 fusion.15
  134.7 2.4 fusion.16
  138.8 9.4 %multiply_reduce_fusion.2 = (f32[64,512]{1,0:T(8,128)S(1)}, f32[64,512]{1,0:T(8,128)S(1)}, f32[64,512]{1,0:T(8,128)S(1)}, f32[64,512]{1,0:T(8,128)S(1)}, f32[64,...) fusion(f32[4,76,524]{2,1,0:T(8,128)S(1)} %get-tuple-element.142, ...), kind=kLoop, calls=%fused_computation.14 | loop fusion | flops 21168128 | bytes 44351488 | tf_op jit(solution)/shard_map/reduce_sum | solution.py:60
  148.3 2.5 multiply_reduce_fusion.39
  150.8 2.4 multiply_reduce_fusion.21
  154.3 0.7 stack.214
  157.9 0.7 stack.219
  164.6 0.7 stack.228
  167.6 0.7 stack.232
  168.3 0.7 stack.233
  172.7 0.9 multiply_reduce_fusion.1
  178.7 0.8 stack.248
  179.4 0.7 stack.249
  183.1 1.0 stack.255
  185.6 28.8 %stack.259 = f32[64,64,512]{2,0,1:T(8,128)} concatenate(f32[1,64,512]{2,0,1:T(1,128)S(1)} %stack.195, f32[1,64,512]{2,0,1:T(1,128)S(1)} %stack.196, f32[1,64,512]{2,0,1:T(1,128)S(1)} %stack.197, f32[1,64,512]{2,0,1:T(1,128)S(1)} %stack.198, f32[1,64,512]{2,0,1:T(1,128)S(1)} %stack.199, f32[1,64,512]{2,0,1:T(1,128)S(1)} %stack.200, f32[1,64,512]{2,0,1:T(1,128)S(1)} %stack.201, ...), dimensions={0} | concatenate | bytes 16777216 | tf_op jit(solution)/shard_map/stack | solution.py:59
  214.3 8.2 %fusion.5 = f32[64,64,512]{2,0,1:T(8,128)S(1)} fusion(f32[64,64,512]{2,0,1:T(8,128)} %stack.259, s32[64]{0:T(128)S(1)} %copy-done.4, s32[64]{0:T(128)S(1)} %copy-done.3, s32[64]{0:T(128)S(1)} %get-tuple-element.146, s32[64]{0:T(128)S(1)} %get-tuple-element.145), kind=kOutput, calls=%fused_computation.207 | convolution fusion | flops 1610625024 | bytes 16778240 | tf_op jit(solution)/shard_map/jk,jyx->kyx/dot_general | solution.py:88
  222.5 8.1 %copy.13 = f32[64,64,512]{2,1,0:T(8,128)} copy(f32[64,64,512]{2,0,1:T(8,128)S(1)} %fusion.5) | data formatting | bytes 16777216 | tf_op jit(solution)/shard_map/jk,jyx->kyx/dot_general | solution.py:88
  230.6 62.9 %all-reduce.3.cloned.1.call-done = f32[64,512]{1,0:T(8,128)} async-done(((f32[64,512]{1,0:T(8,128)}), f32[64,512]{1,0:T(8,128)}) %all-reduce.3.cloned.1.call-update) | async-done | bytes 131088 | tf_op jit(solution)/shard_map/psum | solution.py:93
  293.5 0.9 add_multiply_fusion
  294.4 126.6 %reduce-scatter.2.cloned.1.call-done = f32[4,64,512]{2,1,0:T(8,128)} async-done(((f32[64,64,512]{2,1,0:T(8,128)}), f32[4,64,512]{2,1,0:T(8,128)}) %reduce-scatter.2.cloned.1.call-update) | async-done | bytes 524304 | tf_op jit(solution)/shard_map/reduce_scatter | solution.py:87
  421.0 1.9 divide_add_fusion
  (107 shorter events, 27.9 us)
Async XLA Ops:
  7.2 109.9 %copy-start.3 = (s32[64]{0:T(128)S(1)}, s32[64]{0:T(128)}, u32[]{:S(2)}) copy-start(s32[64]{0:T(128)} %constant.15.clone) | copy-start | bytes 772
  7.2 109.9 %copy-start.4 = (s32[64]{0:T(128)S(1)}, s32[64]{0:T(128)}, u32[]{:S(2)}) copy-start(s32[64]{0:T(128)} %constant.16.clone) | copy-start | bytes 772
  7.2 109.8 %all-gather.2.cloned.1.call-start = ((), (), s32[]{:S(2)}) async-start(), calls=%async_computation.1 | async-start | bytes 8912896 | tf_op jit(solution)/shard_map/all_gather | solution.py:82
  7.9 285.6 %all-reduce.3.cloned.1.call-start = ((), (), s32[]{:S(2)}) async-start(), calls=%async_computation.3 | async-start | bytes 262144 | tf_op jit(solution)/shard_map/psum | solution.py:93
  8.9 4.9 %collective-permute-start = (f32[4,6,512]{2,1,0:T(8,128)S(1)}, f32[4,6,512]{2,1,0:T(8,128)S(1)}, u32[]{:S(2)}, u32[]{:S(2)}) collective-permute-start(f32[4,6,512]{2,1,0:T(8,128)S(1)} %get-tuple-element.143), channel_id=1, source_target_pairs={{0,16},{16,32},{32,48},{48,64},{64,80},{80,96},{96,112},{112,128},... | collective-permute-start | bytes 147464 | tf_op jit(solution)/shard_map/ppermute | solution.py:16
  10.6 4.5 %collective-permute-start.1 = (f32[4,6,512]{2,1,0:T(8,128)S(1)}, f32[4,6,512]{2,1,0:T(8,128)S(1)}, u32[]{:S(2)}, u32[]{:S(2)}) collective-permute-start(f32[4,6,512]{2,1,0:T(8,128)S(1)} %get-tuple-element.144), channel_id=1, source_target_pairs={{16,0},{32,16},{48,32},{64,48},{80,64},{96,80},{112,96},{128,112},... | collective-permute-start | bytes 147464 | tf_op jit(solution)/shard_map/ppermute | solution.py:18
  19.4 401.6 %reduce-scatter.2.cloned.1.call-start = ((), (), s32[]{:S(2)}) async-start(), calls=%async_computation.2 | async-start | bytes 8912896 | tf_op jit(solution)/shard_map/reduce_scatter | solution.py:87
  137.8 1.0 copy-start
  148.3 24.5 %copy-start.1 = (f32[4,64,512]{2,1,0:T(8,128)}, f32[4,64,512]{2,1,0:T(8,128)S(1)}, u32[]{:S(2)}) copy-start(f32[4,64,512]{2,1,0:T(8,128)S(1)} %get-tuple-element.76) | copy-start | bytes 1572868
  230.6 190.4 %copy-start.2 = (f32[4,64,512]{2,1,0:T(8,128)S(1)}, f32[4,64,512]{2,1,0:T(8,128)}, u32[]{:S(2)}) copy-start(f32[4,64,512]{2,1,0:T(8,128)} %param.6) | copy-start | bytes 1572868
Sparse Core Ops, SparseCore 0:
  10.4 106.5 all-gather.1
  119.6 173.7 all-reduce.2
  297.2 123.7 reduce-scatter.1
where the time goes:
time: 434 us; the launch traced here: 430 us
  waiting for transfers between devices  289 us (67%)
  local copies, waits for them, and re-layouts  79 us (18%)
  other arithmetic  22.3 us (5%)
  matrix products  21.6 us (5%)
  between operations  14.6 us (3%)
    reduce_scatter x1, waiting for transfers between devices, on_device(): lax.psum_scatter(jnp.einsum('jk,jyx->kyx', columns, ordered_grad, precisi...  127 us
    all_gather x1, waiting for transfers between devices, on_device(): lax.all_gather(cycle_weight, 'tm', axis=0, tiled=True)  97.1 us
    psum x1, waiting for transfers between devices, on_device(): energy = lax.psum(local_energy, 'tm') / (cycle * frames_all) + 1e-06  62.9 us
    another operation x65, local copies, waits for them, and re-layouts, cycle_passes(): jnp.stack([jnp.sum(error_part * window_of(padded, point, height, width),...  60.1 us
    reduce_sum x4, other arithmetic, cycle_passes(): jnp.sum(error_part * window_of(padded, point, height, width), axis=0)  15.2 us
    dot_general x1, matrix products, reorder(): jnp.einsum('jk,kyx->jyx', selector, weights, precision=lax.Precision.HIGH...  13.4 us
  transfers between devices with their start and end apart: 5, of which 4 were waited for; matrix products, arithmetic and copies ran while one was open for 28% of the time, Pallas kernels for 0%

commit v1 on v0

--- a/solution.py
+++ b/solution.py
@@ -90,7 +90,7 @@
         scatter_dimension=0,
         tiled=True,
     )
-    energy = lax.psum(local_energy, "tm") / (cycle * frames_all) + 1e-06
+    energy = jnp.sum(lax.all_gather(local_energy, "tm"), axis=0) / (cycle * frames_all) + 1e-06
     new_weight = cycle_weight + gradient / (frames_all * energy)[None]
     return (new_weight, error)
 

time: 434 us -> 377 us (0.87)
  waiting for transfers between devices: 289 us -> 231 us
    psum x1 -> x0, waiting for transfers between devices: 62.9 us -> none  [on_device(): energy = lax.psum(local_energy, 'tm') / (cycle * frames_all) + 1e-06]
    reduce_scatter x1, waiting for transfers between devices: 127 us -> 132 us  [on_device(): lax.psum_scatter(jnp.einsum('jk,jyx->kyx', columns, ordered_grad, precisi...]
  transfers between devices with their start and end apart: 5 -> 5, of which waited for: 4 -> 3; matrix products, arithmetic and copies ran while one was open for 28% -> 32% of each run, Pallas kernels for 0% -> 0%
where the time goes in v1:
time: 377 us; the launch traced here: 372 us
  waiting for transfers between devices  231 us (61%)
  local copies, waits for them, and re-layouts  78.4 us (21%)
  other arithmetic  23.2 us (6%)
  matrix products  21.6 us (6%)
  between operations  14.6 us (4%)
    reduce_scatter x1, waiting for transfers between devices, on_device(): lax.psum_scatter(jnp.einsum('jk,jyx->kyx', columns, ordered_grad, precisi...  132 us
    all_gather x1, waiting for transfers between devices, on_device(): lax.all_gather(cycle_weight, 'tm', axis=0, tiled=True)  97.1 us
    another operation x65, local copies, waits for them, and re-layouts, cycle_passes(): jnp.stack([jnp.sum(error_part * window_of(padded, point, height, width),...  59.4 us
    reduce_sum x4, other arithmetic, cycle_passes(): jnp.sum(error_part * window_of(padded, point, height, width), axis=0)  15.2 us
    dot_general x1, matrix products, reorder(): jnp.einsum('jk,kyx->jyx', selector, weights, precision=lax.Precision.HIGH...  13.4 us
    dot_general x1, matrix products, on_device(): jnp.einsum('jk,jyx->kyx', columns, ordered_grad, precision=lax.Precision....  8.15 us
    dot_general x1, local copies, waits for them, and re-layouts, on_device(): jnp.einsum('jk,jyx->kyx', columns, ordered_grad, precision=lax.Precision....  8.08 us
  transfers between devices with their start and end apart: 5, of which 3 were waited for; matrix products, arithmetic and copies ran while one was open for 32% of the time, Pallas kernels for 0%

profile of v1, /device:TPU:4, one launch (start us, length us, event | category | flops | bytes accessed | tf_op | source)
XLA Modules:
  0.0 372.5 jit_solution(12245926401332277306)
XLA Ops:
  8.0 0.9 fusion.19
  8.9 1.7 collective-permute-start
  10.6 1.3 collective-permute-start.1
  11.9 0.8 slice_bitcast_fusion.1
  12.7 1.1 constant_dynamic-update-slice_fusion.1
  13.8 1.4 collective-permute-done.1
  15.1 1.4 multiply_reduce_fusion
  16.5 2.9 slice_add_fusion
  19.9 97.1 %all-gather.4.cloned.1.call-done = f32[64,64,512]{2,1,0:T(8,128)} async-done(((f32[4,64,512]{2,1,0:T(8,128)}), f32[64,64,512]{2,1,0:T(8,128)}) %all-gather.4.cloned.1.call-update) | async-done | bytes 8388624 | tf_op jit(solution)/shard_map/all_gather | solution.py:82
  117.0 13.4 %fusion = f32[64,64,512]{2,0,1:T(8,128)S(1)} fusion(f32[64,64,512]{2,1,0:T(8,128)} %all-gather.4.cloned.1.call-done, s32[64]{0:T(128)S(1)} %copy-done.4, s32[64]{0:T(128)S(1)} %copy-done.3, s32[64]{0:T(128)S(1)} %get-tuple-element.146, s32[64]{0:T(128)S(1)} %get-tuple-element.145), kind=kOutput, calls=%fused_computation | convolution fusion | flops 1610625024 | bytes 16778240 | tf_op jit(solution)/shard_map/jk,kyx->jyx/dot_general | solution.py:45
  130.5 1.9 fusion.17
  132.4 2.3 fusion.15
  134.7 2.5 fusion.16
  138.9 9.4 %multiply_reduce_fusion.2 = (f32[64,512]{1,0:T(8,128)S(1)}, f32[64,512]{1,0:T(8,128)S(1)}, f32[64,512]{1,0:T(8,128)S(1)}, f32[64,512]{1,0:T(8,128)S(1)}, f32[64,...) fusion(f32[4,76,524]{2,1,0:T(8,128)S(1)} %get-tuple-element.142, ...), kind=kLoop, calls=%fused_computation.14 | loop fusion | flops 21168128 | bytes 44351488 | tf_op jit(solution)/shard_map/reduce_sum | solution.py:60
  148.3 2.5 multiply_reduce_fusion.39
  152.3 0.7 stack.218
  154.6 2.4 multiply_reduce_fusion.21
  157.7 0.7 stack.222
  158.4 0.7 stack.223
  165.8 0.8 stack.233
  166.5 0.7 stack.234
  170.2 0.9 multiply_reduce_fusion.1
  172.2 0.7 stack.240
  175.2 0.7 stack.244
  179.6 0.7 stack.250
  182.5 1.0 stack.255
  185.0 28.7 %stack.259 = f32[64,64,512]{2,0,1:T(8,128)} concatenate(f32[1,64,512]{2,0,1:T(1,128)S(1)} %stack.195, f32[1,64,512]{2,0,1:T(1,128)S(1)} %stack.196, f32[1,64,512]{2,0,1:T(1,128)S(1)} %stack.197, f32[1,64,512]{2,0,1:T(1,128)S(1)} %stack.198, f32[1,64,512]{2,0,1:T(1,128)S(1)} %stack.199, f32[1,64,512]{2,0,1:T(1,128)S(1)} %stack.200, f32[1,64,512]{2,0,1:T(1,128)S(1)} %stack.201, ...), dimensions={0} | concatenate | bytes 16777216 | tf_op jit(solution)/shard_map/stack | solution.py:59
  213.7 8.2 %fusion.5 = f32[64,64,512]{2,0,1:T(8,128)S(1)} fusion(f32[64,64,512]{2,0,1:T(8,128)} %stack.259, s32[64]{0:T(128)S(1)} %copy-done.4, s32[64]{0:T(128)S(1)} %copy-done.3, s32[64]{0:T(128)S(1)} %get-tuple-element.146, s32[64]{0:T(128)S(1)} %get-tuple-element.145), kind=kOutput, calls=%fused_computation.207 | convolution fusion | flops 1610625024 | bytes 16778240 | tf_op jit(solution)/shard_map/jk,jyx->kyx/dot_general | solution.py:88
  221.9 8.1 %copy.16 = f32[64,64,512]{2,1,0:T(8,128)} copy(f32[64,64,512]{2,0,1:T(8,128)S(1)} %fusion.5) | data formatting | bytes 16777216 | tf_op jit(solution)/shard_map/jk,jyx->kyx/dot_general | solution.py:88
  230.0 1.8 reduce_sum.659
  231.9 131.9 %reduce-scatter.2.cloned.1.call-done = f32[4,64,512]{2,1,0:T(8,128)} async-done(((f32[64,64,512]{2,1,0:T(8,128)}), f32[4,64,512]{2,1,0:T(8,128)}) %reduce-scatter.2.cloned.1.call-update) | async-done | bytes 524304 | tf_op jit(solution)/shard_map/reduce_scatter | solution.py:87
  363.8 1.9 divide_add_fusion
  (108 shorter events, 26.5 us)
Async XLA Ops:
  7.2 109.9 %copy-start.3 = (s32[64]{0:T(128)S(1)}, s32[64]{0:T(128)}, u32[]{:S(2)}) copy-start(s32[64]{0:T(128)} %constant.15.clone) | copy-start | bytes 772
  7.2 109.9 %copy-start.4 = (s32[64]{0:T(128)S(1)}, s32[64]{0:T(128)}, u32[]{:S(2)}) copy-start(s32[64]{0:T(128)} %constant.16.clone) | copy-start | bytes 772
  7.2 109.8 %all-gather.4.cloned.1.call-start = ((), (), s32[]{:S(2)}) async-start(), calls=%async_computation.1 | async-start | bytes 8912896 | tf_op jit(solution)/shard_map/all_gather | solution.py:82
  7.9 222.1 %all-gather.6.cloned.1.call-start = ((), (), s32[]{:S(2)}) async-start(), calls=%async_computation.3 | async-start | bytes 2228224 | tf_op jit(solution)/shard_map/all_gather | solution.py:93
  8.9 4.9 %collective-permute-start = (f32[4,6,512]{2,1,0:T(8,128)S(1)}, f32[4,6,512]{2,1,0:T(8,128)S(1)}, u32[]{:S(2)}, u32[]{:S(2)}) collective-permute-start(f32[4,6,512]{2,1,0:T(8,128)S(1)} %get-tuple-element.143), channel_id=1, source_target_pairs={{0,16},{16,32},{32,48},{48,64},{64,80},{80,96},{96,112},{112,128},... | collective-permute-start | bytes 147464 | tf_op jit(solution)/shard_map/ppermute | solution.py:16
  10.6 4.5 %collective-permute-start.1 = (f32[4,6,512]{2,1,0:T(8,128)S(1)}, f32[4,6,512]{2,1,0:T(8,128)S(1)}, u32[]{:S(2)}, u32[]{:S(2)}) collective-permute-start(f32[4,6,512]{2,1,0:T(8,128)S(1)} %get-tuple-element.144), channel_id=1, source_target_pairs={{16,0},{32,16},{48,32},{64,48},{80,64},{96,80},{112,96},{128,112},... | collective-permute-start | bytes 147464 | tf_op jit(solution)/shard_map/ppermute | solution.py:18
  19.4 344.4 %reduce-scatter.2.cloned.1.call-start = ((), (), s32[]{:S(2)}) async-start(), calls=%async_computation.2 | async-start | bytes 8912896 | tf_op jit(solution)/shard_map/reduce_scatter | solution.py:87
  137.8 1.0 copy-start
  148.3 21.9 %copy-start.1 = (f32[4,64,512]{2,1,0:T(8,128)}, f32[4,64,512]{2,1,0:T(8,128)S(1)}, u32[]{:S(2)}) copy-start(f32[4,64,512]{2,1,0:T(8,128)S(1)} %get-tuple-element.76) | copy-start | bytes 1572868
  230.0 133.8 %copy-start.2 = (f32[4,64,512]{2,1,0:T(8,128)S(1)}, f32[4,64,512]{2,1,0:T(8,128)}, u32[]{:S(2)}) copy-start(f32[4,64,512]{2,1,0:T(8,128)} %param.6) | copy-start | bytes 1572868
Sparse Core Ops, SparseCore 0:
  10.4 106.5 all-gather.3
  119.5 70.7 all-gather.5
  230.1 133.6 reduce-scatter.1
